TPU v7x, 256 devices: a whole 4x4x8 slice. The times are simulated.
256 devices in a mesh: prow: 8 (over y, core), pcol: 32 (over x, z).
Axes of the slice: x: 4, y: 4, z: 8, core: 2. Of those that a mesh axis runs over, the one named last changes fastest.
Arguments:
- diag_one: float32 [1024, 1024], P('pcol')
- top_rows: bfloat16 [1024, 1024], P('pcol'), may hold values from -0.1875 to 0.1875
- panel_one: bfloat16 [131072, 1024], P(('prow', 'pcol')), may hold values from -6 to 6
- first_block: int32 [512], P(('prow', 'pcol')), may hold values from 0 to 3
- target: int32 [512], P(('prow', 'pcol')), may hold values from 0 to 511, as said below
- diag_two: float32 [1024, 1024], P('pcol'), may hold values from -6 to 6
- panel_two: bfloat16 [131072, 1024], P(('prow', 'pcol')), may hold values from -6 to 6
Outputs:
- panel_factor: bfloat16 [131072, 1024], P(('prow', 'pcol'))
- top_factor: bfloat16 [1024, 1024], P('pcol')
- diag_next: float32 [1024, 1024], P('pcol')
- panel_next: float32 [131072, 1024], P(('prow', 'pcol'))
Inputs may be any that keep to these rules, and one draw needn't show every extreme that they name: Row block t of the second supernode is held by grid row (t // 2) // 32 and grid column (t // 2) % 32; target[i] lies in the grid column of row block i; the 2 row blocks of one device go to 2 different grid rows; in every grid column one grid row receives a row block from every grid row.
All inputs are finite; a program needn't handle non-finite values.
Results may differ from a plain program's by a relative error of at most 0.0021.
Values may be sent and summed in bfloat16 or wider, within the bound.
A program may use at most 128 MiB of HBM per device.

v0:
```python
import functools

import jax
import jax.numpy as jnp
from jax import lax
from jax.experimental import pallas as pl
from jax.experimental.pallas import tpu as pltpu
from jax.sharding import PartitionSpec as P

F32, BF16 = jnp.float32, jnp.bfloat16
NB = 128


def split2(x):
    hi = x.astype(BF16)
    lo = (x - hi.astype(F32)).astype(BF16)
    return hi, lo


def tdot(left, right):
    return lax.dot_general(left, right, (((0,), (0,)), ((), ())), preferred_element_type=F32)


def row_bcast(x, k):
    return jnp.broadcast_to(x[k:k + 1, :], (8, x.shape[1]))


def factor_block(m_ref, t_ref, G):
    n = NB
    sub = lax.broadcasted_iota(jnp.int32, (8, n), 0)
    lane = lax.broadcasted_iota(jnp.int32, (8, n), 1)
    for s in range(n // G):
        r0 = s * G
        nch = G // 8
        raw = [m_ref[r0 + 8 * c:r0 + 8 * c + 8, :] for c in range(nch)]
        cols = {}
        for j in range(G):
            for c in range(j // 8, nch):
                cols[j, c] = jnp.broadcast_to(raw[c][:, r0 + j:r0 + j + 1], (8, n))
        inside = (lane >= r0) & (lane < r0 + G)
        band = [
            jnp.where(inside, (lane == sub + (r0 + 8 * c)).astype(F32), raw[c]) for c in range(nch)
        ]
        dvec = [None] * nch
        for k in range(G):
            kc, kr = k // 8, k % 8
            piv = row_bcast(cols[k, kc], kr)
            dvec[kc] = piv if kr == 0 else jnp.where(sub >= kr, piv, dvec[kc])
            rd = 1.0 / piv
            mult = {}
            for c in range(kc, nch):
                mult[c] = cols[k, c] * rd
            mult[kc] = jnp.where(sub > kr, mult[kc], 0.0)
            for j in range(k + 1, G):
                jc = j // 8
                other = row_bcast(cols[k, jc], j % 8)
                for c in range(jc, nch):
                    cols[j, c] = cols[j, c] - mult[c] * other
            row = row_bcast(band[kc], kr)
            for c in range(kc, nch):
                band[c] = band[c] - mult[c] * row
        band = [band[c] * lax.rsqrt(dvec[c]) for c in range(nch)]
        for c in range(nch):
            t_ref[r0 + 8 * c:r0 + 8 * c + 8, :] = jnp.where(lane < r0 + G, band[c], 0.0)
        if r0 + G < n:
            r = jnp.concatenate(band, axis=0)
            hi, lo = split2(r)
            prod = tdot(jnp.concatenate([hi, hi, lo], axis=0), jnp.concatenate([hi, lo, hi], axis=0))
            lane_all = lax.broadcasted_iota(jnp.int32, (n - r0 - G, n), 1)
            keep = (lane_all < r0) | (lane_all >= r0 + G)
            m_ref[r0 + G:, :] = jnp.where(keep, m_ref[r0 + G:, :], 0.0) - prod[r0 + G:, :]


def chol_kernel(G, a_ref, hi_ref, lo_ref, w, m, t, left, right):
    n = w.shape[0]
    steps = n // NB
    w[...] = a_ref[...]

    def step(b, carry):
        o = pl.multiple_of(b * NB, NB)
        mine = pl.ds(o, NB)
        m[...] = w[mine, mine]
        factor_block(m, t, G)
        th, tl = split2(t[...])
        wh, wl = split2(w[mine, :])
        r = jnp.dot(jnp.concatenate([th, th, tl], axis=1), jnp.concatenate([wh, wl, wh], axis=0),
                    preferred_element_type=F32)
        w[mine, :] = r
        w[mine, mine] = t[...]
        rh, rl = split2(w[mine, :])
        left[0:NB, :] = rh
        left[NB:2 * NB, :] = rh
        left[2 * NB:, :] = rl
        right[0:NB, :] = rh
        right[NB:2 * NB, :] = rl
        right[2 * NB:, :] = rh
        done = lax.broadcasted_iota(jnp.int32, (NB, n), 1) < o + NB
        hi_ref[mine, :] = jnp.where(done, rh, jnp.zeros_like(rh))
        lo_ref[mine, :] = jnp.where(done, rl, jnp.zeros_like(rl))

        def trail(i, carry):
            below = pl.ds(pl.multiple_of(i * NB, NB), NB)
            w[below, mine] = jnp.zeros((NB, NB), F32)
            w[below, :] = w[below, :] - tdot(left[:, below], right[...])
            return carry

        lax.fori_loop(b + 1, steps, trail, 0)
        return carry

    lax.fori_loop(0, steps, step, 0)


def inverse_factor(a):
    n = a.shape[0]
    whole = pl.BlockSpec(memory_space=pltpu.VMEM)
    return pl.pallas_call(
        functools.partial(chol_kernel, 32),
        out_shape=[jax.ShapeDtypeStruct((n, n), BF16)] * 2,
        in_specs=[whole],
        out_specs=[whole] * 2,
        scratch_shapes=[
            pltpu.VMEM((n, n), F32),
            pltpu.VMEM((NB, NB), F32),
            pltpu.VMEM((NB, NB), F32),
            pltpu.VMEM((3 * NB, n), BF16),
            pltpu.VMEM((3 * NB, n), BF16),
        ],
        compiler_params=pltpu.CompilerParams(vmem_limit_bytes=40 << 20),
        cost_estimate=pl.CostEstimate(flops=40 * n**3, bytes_accessed=8 * n * n, transcendentals=0),
    )(a)


def ndot(left, right):
    return lax.dot_general(left, right, (((1,), (1,)), ((), ())), preferred_element_type=F32)


def solve_into(rows, hi_ref, lo_ref, store):
    n = hi_ref.shape[0]
    for j in range(n // 256):
        cut = slice(256 * j, 256 * j + 256)
        upto = slice(0, 256 * j + 256)
        part = rows[:, upto]
        out = ndot(part, hi_ref[cut, upto]) + ndot(part, lo_ref[cut, upto])
        store(cut, out.astype(BF16))


def apply_kernel(
    tops, owns, info, hi_ref, lo_ref, top_ref, own_ref, inc_ref, two_ref, diag_ref,
    pf_ref, tf_ref, dn_ref, pn_ref, tf, solved,
):
    i = pl.program_id(0)
    rows, n = top_ref.shape

    @pl.when(i == 0)
    def _():
        pn_ref[...] = two_ref[...].astype(F32)

    @pl.when(i < tops)
    def _():
        at = pl.ds(pl.multiple_of(i * rows, rows), rows)

        def store(cut, value):
            tf[at, cut] = value

        solve_into(top_ref[...], hi_ref, lo_ref, store)

    @pl.when((i >= tops) & (i < tops + owns))
    def _():
        column = lax.broadcasted_iota(jnp.int32, (rows, n), 1)
        x = own_ref[...].astype(F32)
        x = jnp.where(column >= info[1 + i - tops] * rows, x, 0.0).astype(BF16)

        def store(cut, value):
            pf_ref[:, cut] = value

        solve_into(x, hi_ref, lo_ref, store)

    @pl.when(i == tops)
    def _():
        local = tf_ref.shape[0]
        own = tf[pl.ds(pl.multiple_of(info[0] * local, local), local), :]
        tf_ref[...] = own
        dn_ref[...] = diag_ref[...] - ndot(own, tf[...])

    @pl.when(i >= tops + owns)
    def _():
        slot = info[1 + owns + i - tops - owns]

        @pl.when(slot >= 0)
        def _():
            def store(cut, value):
                solved[:, cut] = value

            solve_into(inc_ref[0], hi_ref, lo_ref, store)
            at = pl.ds(pl.multiple_of(slot * rows, rows), rows)
            update = ndot(solved[...], tf[...]).astype(BF16).astype(F32)
            pn_ref[at, :] = pn_ref[at, :] - update


def apply(info, hi, lo, top, own, incoming, two, diag_two):
    n = hi.shape[0]
    sources, rows, _ = incoming.shape
    tops, owns = n // rows, own.shape[0] // rows
    local = diag_two.shape[0]
    fixed = lambda *shape: pl.BlockSpec(shape, lambda i, info: (0,) * len(shape))
    clip = lambda i, low, count: jnp.minimum(jnp.maximum(i - low, 0), count - 1)
    return pl.pallas_call(
        functools.partial(apply_kernel, tops, owns),
        out_shape=[
            jax.ShapeDtypeStruct(own.shape, BF16),
            jax.ShapeDtypeStruct((local, n), BF16),
            jax.ShapeDtypeStruct((local, n), F32),
            jax.ShapeDtypeStruct(two.shape, F32),
        ],
        grid_spec=pltpu.PrefetchScalarGridSpec(
            num_scalar_prefetch=1,
            grid=(tops + owns + sources,),
            in_specs=[
                fixed(n, n), fixed(n, n),
                pl.BlockSpec((rows, n), lambda i, info: (clip(i, 0, tops), 0)),
                pl.BlockSpec((rows, n), lambda i, info: (clip(i, tops, owns), 0)),
                pl.BlockSpec((1, rows, n), lambda i, info: (clip(i, tops + owns, sources), 0, 0)),
                fixed(*two.shape), fixed(local, n),
            ],
            out_specs=[
                pl.BlockSpec((rows, n), lambda i, info: (clip(i, tops, owns), 0)),
                fixed(local, n), fixed(local, n), fixed(*two.shape),
            ],
            scratch_shapes=[pltpu.VMEM((n, n), BF16), pltpu.VMEM((rows, n), BF16)],
        ),
        compiler_params=pltpu.CompilerParams(vmem_limit_bytes=48 << 20),
    )(info, hi, lo, top, own, incoming, two, diag_two)


def on_device(diag_one, top_rows, panel_one, first_block, target, diag_two, panel_two):
    n = diag_one.shape[1]
    blocks = first_block.shape[0]
    rows = panel_one.shape[0] // blocks
    grid_rows = lax.axis_size("prow")
    grid_cols = lax.axis_size("pcol")
    whole_diag = lax.all_gather(diag_one, "pcol", axis=0, tiled=True)
    whole_top = lax.all_gather(top_rows, "pcol", axis=0, tiled=True)
    dest_row = target // (blocks * grid_cols)
    dest_slot = target % blocks
    routing = dest_row[None, :] == jnp.arange(grid_rows, dtype=jnp.int32)[:, None]
    send_slot = jnp.sum(jnp.where(routing, dest_slot[None, :] + 1, 0), axis=1) - 1
    column = jnp.arange(n, dtype=jnp.int32)[None, :] // rows
    zero = jnp.zeros((), BF16)
    outgoing = jnp.zeros((grid_rows, rows, n), BF16)
    for r in range(blocks):
        piece = panel_one[r * rows:(r + 1) * rows]
        piece = jnp.where(column >= first_block[r], piece, zero)
        outgoing = jnp.where(routing[:, r][:, None, None], piece[None], outgoing)
    incoming = lax.all_to_all(outgoing, "prow", split_axis=0, concat_axis=0, tiled=True)
    incoming_slot = lax.all_to_all(send_slot, "prow", split_axis=0, concat_axis=0, tiled=True)
    info = jnp.concatenate(
        [lax.axis_index("pcol").astype(jnp.int32)[None], first_block, incoming_slot]
    )
    hi, lo = inverse_factor(whole_diag)
    panel_factor, top_own, diag_next, panel_next = apply(
        info, hi, lo, whole_top, panel_one, incoming, panel_two, diag_two
    )
    return (panel_factor, top_own, diag_next, panel_next)


def solution(mesh):
    whole = P(("prow", "pcol"), None)
    blocks = P(("prow", "pcol"))
    part = P("pcol", None)
    return jax.shard_map(
        on_device,
        mesh=mesh,
        in_specs=(part, part, whole, blocks, blocks, part, whole),
        out_specs=(whole, part, part, whole),
        check_vma=False,
    )
```

profile of v0, /device:TPU:2, one launch (start us, length us, event | category | flops | bytes accessed | tf_op | source)
XLA Modules:
  0.0 205.9 jit_solution(12645084085889379635)
XLA Ops:
  7.2 0.0 all-gather.3.cloned.1.call-start
  7.2 0.7 all-gather.3.cloned.1.call-update
  7.9 0.7 and_select_fusion.1
  8.6 0.1 select_reduce_fusion
  8.7 0.7 copy.12
  9.3 4.5 %all-to-all-start = ((s32[8,1,1]{2,1,0:T(1,128)}), s32[8,1,1]{2,1,0:T(1,128)S(1)}, u32[]{:S(2)}, u32[]{:S(2)}) async-start(s32[8,1,1]{2,1,0:T(1,128)} %copy.12), calls=%async_computation | async-start | bytes 8192 | tf_op jit(solution)/shard_map/all_to_all | solution.py:255
  13.8 0.0 all-gather.5.cloned.1.call-start
  13.9 0.7 all-gather.5.cloned.1.call-update
  14.6 0.1 iota_compare_fusion
  14.6 1.3 fusion.6
  16.0 1.3 fusion.2
  17.3 1.3 slice_select_fusion.1
  18.5 2.6 %select_select_fusion = bf16[8,256,1024]{2,1,0:T(8,128)(2,1)} fusion(pred[8]{0:T(512)(128)(4,1)S(1)} %get-tuple-element.13, pred[8]{0:T(512)(128)(4,1)S(1)} %get-tuple-element.12, bf16[256,1024]{1,0:T(8,128)(2,1)S(1)} %get-tuple-element.9, bf16[256,1024]{1,0:T(8,128)(2,1)S(1)} %get-tuple-element.8), kind=kLoop, calls=%fused_computation | loop fusion | flops 4194304 | bytes 5242896 | tf_op jit(solution)/shard_map/jit(_where)/select_n | solution.py:253
  21.1 0.0 copy-start.5
  21.1 0.0 all-to-all-done
  21.1 4.9 %all-to-all-start.1 = ((bf16[8,256,1024]{2,1,0:T(8,128)(2,1)}), bf16[8,256,1024]{2,1,0:T(8,128)(2,1)}, u32[]{:S(2)}, u32[]{:S(2)}) async-start(bf16[8,256,1024]{2,1,0:T(8,128)(2,1)} %select_select_fusion), calls=%async_computation.1 | async-start | bytes 8388608 | tf_op jit(solution)/shard_map/all_to_all | solution.py:254
  26.0 0.2 reduce
  26.3 0.0 copy-done.5
  26.3 0.1 pad_add_fusion.info
  26.4 0.0 copy-start
  26.4 0.0 copy-start.3
  26.4 67.7 %all-gather.3.cloned.1.call-done.a_ref = f32[1024,1024]{1,0:T(8,128)} async-done(((f32[32,1024]{1,0:T(8,128)}), f32[1024,1024]{1,0:T(8,128)}) %all-gather.3.cloned.1.call-update) | async-done | bytes 4194320 | tf_op jit(solution)/shard_map/all_gather | solution.py:241
  94.0 2.2 %copy-done.4 = f32[1024,1024]{1,0:T(8,128)S(1)} copy-done((f32[1024,1024]{1,0:T(8,128)S(1)}, f32[1024,1024]{1,0:T(8,128)}, u32[]{:S(2)}) %copy-start.4) | copy-done | bytes 4194328
  96.2 36.2 %shard_map.102 = (bf16[1024,1024]{1,0:T(8,128)(2,1)S(1)}, bf16[1024,1024]{1,0:T(8,128)(2,1)S(1)}) custom-call(f32[1024,1024]{1,0:T(8,128)S(1)} %copy-done.4), custom_call_target="tpu_custom_call" | custom-call | flops 42949672960 | bytes 8388608 | tf_op jit(solution)/shard_map/pallas_call | solution.py:116
  132.4 0.0 copy-start.1
  132.5 1.3 copy-done.1
  133.8 0.0 all-to-all-done.1.inc_ref
  133.8 38.1 %all-gather.5.cloned.1.call-done.top_ref = bf16[1024,1024]{1,0:T(8,128)(2,1)} async-done(((bf16[32,1024]{1,0:T(8,128)(2,1)}), bf16[1024,1024]{1,0:T(8,128)(2,1)}) %all-gather.5.cloned.1.call-update) | async-done | bytes 2097168 | tf_op jit(solution)/shard_map/all_gather | solution.py:242
  171.9 0.0 copy-done
  171.9 0.0 copy-done.3
  171.9 1.2 copy-done.2
  173.1 25.9 %shard_map.103 = (bf16[512,1024]{1,0:T(8,128)(2,1)}, bf16[32,1024]{1,0:T(8,128)(2,1)}, f32[32,1024]{1,0:T(8,128)}, f32[512,1024]{1,0:T(8,128)}) custom-call(s32[11]{0:T(128)S(1)} %pad_add_fusion.info, bf16[1024,1024]{1,0:T(8,128)(2,1)S(1)} %get-tuple-element.6.hi_ref, bf16[1024,1024]{1,0:T(8,128)(2,1)} %copy-done.1, ...), custom_call_target="tpu_custom_call" | custom-call | tf_op jit(solution)/shard_map/pallas_call | solution.py:207
  (4 shorter events, 0.0 us)
Async XLA Ops:
  7.2 86.9 %all-gather.3.cloned.1.call-start = ((), (), s32[]{:S(2)}) async-start(), calls=%async_computation.2 | async-start | bytes 4325376 | tf_op jit(solution)/shard_map/all_gather | solution.py:241
  9.3 11.8 %all-to-all-start = ((s32[8,1,1]{2,1,0:T(1,128)}), s32[8,1,1]{2,1,0:T(1,128)S(1)}, u32[]{:S(2)}, u32[]{:S(2)}) async-start(s32[8,1,1]{2,1,0:T(1,128)} %copy.12), calls=%async_computation | async-start | bytes 8192 | tf_op jit(solution)/shard_map/all_to_all | solution.py:255
  13.8 158.1 %all-gather.5.cloned.1.call-start = ((), (), s32[]{:S(2)}) async-start(), calls=%async_computation.3 | async-start | bytes 2162688 | tf_op jit(solution)/shard_map/all_gather | solution.py:242
  21.1 5.2 %copy-start.5 = (s32[2]{0:T(128)S(1)}, s32[2]{0:T(128)}, u32[]{:S(2)}) copy-start(s32[2]{0:T(128)} %param.10) | copy-start | bytes 28
  21.1 112.7 %all-to-all-start.1 = ((bf16[8,256,1024]{2,1,0:T(8,128)(2,1)}), bf16[8,256,1024]{2,1,0:T(8,128)(2,1)}, u32[]{:S(2)}, u32[]{:S(2)}) async-start(bf16[8,256,1024]{2,1,0:T(8,128)(2,1)} %select_select_fusion), calls=%async_computation.1 | async-start | bytes 8388608 | tf_op jit(solution)/shard_map/all_to_all | solution.py:254
  26.4 145.5 %copy-start = (bf16[512,1024]{1,0:T(8,128)(2,1)S(1)}, bf16[512,1024]{1,0:T(8,128)(2,1)}, u32[]{:S(2)}) copy-start(bf16[512,1024]{1,0:T(8,128)(2,1)} %own_ref.1) | copy-start | bytes 3145732
  26.4 145.5 %copy-start.3 = (f32[32,1024]{1,0:T(8,128)S(1)}, f32[32,1024]{1,0:T(8,128)}, u32[]{:S(2)}) copy-start(f32[32,1024]{1,0:T(8,128)} %diag_ref.1) | copy-start | bytes 393220
  94.0 2.2 %copy-start.4 = (f32[1024,1024]{1,0:T(8,128)S(1)}, f32[1024,1024]{1,0:T(8,128)}, u32[]{:S(2)}) copy-start(f32[1024,1024]{1,0:T(8,128)} %all-gather.3.cloned.1.call-done.a_ref) | copy-start | bytes 12582916
  132.4 1.4 copy-start.1
  171.9 1.2 copy-start.2
Sparse Core Ops, SparseCore 0:
  10.6 83.4 all-gather.2
  96.6 75.2 all-gather.4
where the time goes:
time: 206 us
  waiting for transfers between devices  107 us (52%)
  Pallas kernels  62.1 us (30%)
  between operations  14.1 us (7%)
  starting transfers between devices  9.47 us (5%)
  local copies, waits for them, and re-layouts  6.77 us (3%)
  other arithmetic  6.3 us (3%)
    all_gather x1, waiting for transfers between devices, on_device(): whole_diag = lax.all_gather(diag_one, 'pcol', axis=0, tiled=True)  67.7 us
    all_gather x1, waiting for transfers between devices, on_device(): whole_top = lax.all_gather(top_rows, 'pcol', axis=0, tiled=True)  38.1 us
    pallas_call x1, Pallas kernels, inverse_factor(): pl.pallas_call(functools.partial(chol_kernel, 32), out_shape=[jax.ShapeDt...  36.2 us
    pallas_call x1, Pallas kernels, apply(): pl.pallas_call(functools.partial(apply_kernel, tops, owns), out_shape=[ja...  25.9 us
    all_to_all x1, starting transfers between devices, on_device(): lax.all_to_all(outgoing, 'prow', split_axis=0, concat_axis=0, tiled=True)  4.92 us
    unnamed x12, local copies, waits for them, and re-layouts  4.77 us
    all_to_all x1, starting transfers between devices, on_device(): lax.all_to_all(send_slot, 'prow', split_axis=0, concat_axis=0, tiled=True)  4.47 us
  transfers between devices with their start and end apart: 4, of which 2 were waited for; matrix products, arithmetic and copies ran while one was open for 4% of the time, Pallas kernels for 18%

commit v1 on v0

v1 whole, which is shorter than its diff:
```python
import functools

import jax
import jax.numpy as jnp
from jax import lax
from jax.experimental import pallas as pl
from jax.experimental.pallas import tpu as pltpu
from jax.sharding import PartitionSpec as P

F32, BF16 = jnp.float32, jnp.bfloat16
NB = 128


def split2(x):
    hi = x.astype(BF16)
    lo = (x - hi.astype(F32)).astype(BF16)
    return hi, lo


def tdot(left, right):
    return lax.dot_general(left, right, (((0,), (0,)), ((), ())), preferred_element_type=F32)


def row_bcast(x, k):
    return jnp.broadcast_to(x[k:k + 1, :], (8, x.shape[1]))


def factor_block(m_ref, t_ref, G):
    n = NB
    sub = lax.broadcasted_iota(jnp.int32, (8, n), 0)
    lane = lax.broadcasted_iota(jnp.int32, (8, n), 1)
    for s in range(n // G):
        r0 = s * G
        nch = G // 8
        raw = [m_ref[r0 + 8 * c:r0 + 8 * c + 8, :] for c in range(nch)]
        cols = {}
        for j in range(G):
            for c in range(j // 8, nch):
                cols[j, c] = jnp.broadcast_to(raw[c][:, r0 + j:r0 + j + 1], (8, n))
        inside = (lane >= r0) & (lane < r0 + G)
        band = [
            jnp.where(inside, (lane == sub + (r0 + 8 * c)).astype(F32), raw[c]) for c in range(nch)
        ]
        dvec = [None] * nch
        for k in range(G):
            kc, kr = k // 8, k % 8
            piv = row_bcast(cols[k, kc], kr)
            dvec[kc] = piv if kr == 0 else jnp.where(sub >= kr, piv, dvec[kc])
            rd = 1.0 / piv
            mult = {}
            for c in range(kc, nch):
                mult[c] = cols[k, c] * rd
            mult[kc] = jnp.where(sub > kr, mult[kc], 0.0)
            for j in range(k + 1, G):
                jc = j // 8
                other = row_bcast(cols[k, jc], j % 8)
                for c in range(jc, nch):
                    cols[j, c] = cols[j, c] - mult[c] * other
            row = row_bcast(band[kc], kr)
            for c in range(kc, nch):
                band[c] = band[c] - mult[c] * row
        band = [band[c] * lax.rsqrt(dvec[c]) for c in range(nch)]
        for c in range(nch):
            t_ref[r0 + 8 * c:r0 + 8 * c + 8, :] = jnp.where(lane < r0 + G, band[c], 0.0)
        if r0 + G < n:
            r = jnp.concatenate(band, axis=0)
            hi, lo = split2(r)
            prod = tdot(jnp.concatenate([hi, hi, lo], axis=0), jnp.concatenate([hi, lo, hi], axis=0))
            lane_all = lax.broadcasted_iota(jnp.int32, (n - r0 - G, n), 1)
            keep = (lane_all < r0) | (lane_all >= r0 + G)
            m_ref[r0 + G:, :] = jnp.where(keep, m_ref[r0 + G:, :], 0.0) - prod[r0 + G:, :]


NX, NZ = 4, 8
MESH = pl.DeviceIdType.MESH


def eliminate(b, w, m, t, left, right, hi_ref, lo_ref):
    n = w.shape[1]
    o = pl.multiple_of(b * NB, NB)
    mine = pl.ds(o, NB)
    m[...] = w[mine, mine]
    factor_block(m, t, 32)
    th, tl = split2(t[...])
    wh, wl = split2(w[mine, :])
    r = jnp.dot(
        jnp.concatenate([th, th, tl], axis=1),
        jnp.concatenate([wh, wl, wh], axis=0),
        preferred_element_type=F32,
    )
    w[mine, :] = r
    w[mine, mine] = t[...]
    rh, rl = split2(w[mine, :])
    left[0:NB, :] = rh
    left[NB:2 * NB, :] = rh
    left[2 * NB:, :] = rl
    right[0:NB, :] = rh
    right[NB:2 * NB, :] = rl
    right[2 * NB:, :] = rh
    done = lax.broadcasted_iota(jnp.int32, (NB, n), 1) < o + NB
    hi_ref[mine, :] = jnp.where(done, rh, jnp.zeros_like(rh))
    lo_ref[mine, :] = jnp.where(done, rl, jnp.zeros_like(rl))

    def trail(i, carry):
        below = pl.ds(pl.multiple_of(i * NB, NB), NB)
        w[below, mine] = jnp.zeros((NB, NB), F32)
        w[below, :] = w[below, :] - tdot(left[:, below], right[...])
        return carry

    lax.fori_loop(b + 1, n // NB, trail, 0)


class Ring:
    def __init__(self, own, whole, sems, trim):
        self.own, self.whole, self.trim = own, whole, trim
        self.xsend, self.xrecv, self.zsend, self.zrecv, self.ssend, self.srecv = sems
        self.rows, self.n = own.shape
        self.prow, pcol = lax.axis_index("prow"), lax.axis_index("pcol")
        self.core = lax.rem(self.prow, 2)
        self.x, self.z = pcol // NZ, lax.rem(pcol, NZ)
        self.sibling = (self.prow + 1 - 2 * self.core, pcol)
        self.hops = (NZ // 2, NZ // 2 - 1)

    def at(self, x, z):
        return (self.prow, lax.rem(x + NX, NX) * NZ + lax.rem(z + NZ, NZ))

    def place(self, xs, zz):
        skip = self.n // NX * xs if self.trim else 0
        width = (self.n - skip) // 2
        row = pl.multiple_of((xs * NZ + zz) * self.rows, self.rows)
        return pl.ds(row, self.rows), pl.ds(pl.multiple_of(skip + self.core * width, 128), width)

    def xcopy(self, xs, d):
        where = self.place(xs, self.z)
        return pltpu.make_async_remote_copy(
            self.own.at[:, where[1]], self.whole.at[where], self.xsend.at[d - 1], self.xrecv.at[xs],
            device_id=self.at(xs + d, self.z), device_id_type=MESH,
        )

    def scopy(self, xs, zz, slot):
        where = self.whole.at[self.place(xs, zz)]
        return pltpu.make_async_remote_copy(
            where, where, self.ssend.at[xs, slot], self.srecv.at[xs, slot],
            device_id=self.sibling, device_id_type=MESH,
        )

    def zcopy(self, xs, zz, way, hop):
        where = self.whole.at[self.place(xs, zz)]
        return pltpu.make_async_remote_copy(
            where, where, self.zsend.at[xs, way, hop], self.zrecv.at[xs, way, hop],
            device_id=self.at(self.x, self.z + 1 - 2 * way), device_id_type=MESH,
        )

    def start(self):
        for xs in range(NX):
            @pl.when(self.x == xs)
            def _():
                for d in range(1, NX):
                    self.xcopy(xs, d).start()

    def across(self):
        for xs in range(NX):
            @pl.when(self.x != xs)
            def _():
                self.xcopy(xs, 1).wait_recv()
            for way in range(2):
                self.zcopy(xs, self.z, way, 0).start()
        for xs in range(NX):
            @pl.when(self.x != xs)
            def _():
                self.scopy(xs, self.z, 0).start()

    def hop(self, hop):
        for way in range(2):
            if hop >= self.hops[way]:
                continue
            back = self.z - hop - 1 if way == 0 else self.z + hop + 1
            back = lax.rem(back + NZ, NZ)
            for xs in range(NX):
                self.zcopy(xs, back, way, hop).wait_recv()
                if hop + 1 < self.hops[way]:
                    self.zcopy(xs, back, way, hop + 1).start()
                self.scopy(xs, back, 1 + hop + way * (NZ // 2)).start()

    def finish(self):
        for xs in range(NX):
            @pl.when(self.x != xs)
            def _():
                self.scopy(xs, self.z, 0).wait_recv()
            for slot in range(1, NZ):
                self.scopy(xs, self.z, slot).wait_recv()

    def drain(self):
        for xs in range(NX):
            @pl.when(self.x == xs)
            def _():
                for d in range(1, NX):
                    self.xcopy(xs, d).wait_send()

            @pl.when(self.x != xs)
            def _():
                self.scopy(xs, self.z, 0).wait_send()
            for way in range(2):
                for hop in range(self.hops[way]):
                    self.zcopy(xs, self.z, way, hop).wait_send()
            for slot in range(1, NZ):
                self.scopy(xs, self.z, slot).wait_send()


def factor_kernel(
    first_ref, target_ref, diag_ref, top_ref, panel_ref,
    hi_ref, lo_ref, tops_ref, inc_ref, marks_ref,
    w, m, t, left, right, panel, outgoing, mark, local, *sems,
):
    grid_rows, rows, n = inc_ref.shape
    blocks = panel.shape[0] // rows
    diag = Ring(diag_ref, w, sems[0:6], True)
    top = Ring(top_ref, tops_ref, sems[6:12], False)
    psend, precv, msend, mrecv = sems[12:]
    prow, pcol = diag.prow, lax.axis_index("pcol")
    own_rows = pl.ds(pl.multiple_of(pcol * diag.rows, diag.rows), diag.rows)

    barrier = pltpu.get_barrier_semaphore()
    peers = [diag.at(diag.x + d, diag.z) for d in range(1, NX)]
    peers += [diag.at(diag.x, diag.z + 1), diag.at(diag.x, diag.z - 1)]
    peers += [(lax.rem(prow + d, grid_rows), pcol) for d in range(1, grid_rows)]
    for peer in peers:
        pl.semaphore_signal(barrier, inc=1, device_id=peer, device_id_type=MESH)
    load = pltpu.make_async_copy(panel_ref, panel, local.at[0])
    load.start()
    keep_diag = pltpu.make_async_copy(diag_ref, w.at[own_rows], local.at[1])
    keep_diag.start()
    keep_top = pltpu.make_async_copy(top_ref, tops_ref.at[own_rows], local.at[2])
    keep_top.start()
    pl.semaphore_wait(barrier, len(peers))

    diag.start()
    lane = lax.broadcasted_iota(jnp.int32, mark.shape, 1)
    mark[...] = jnp.where(lane == 0, target_ref[0], target_ref[1])
    load.wait()
    column = lax.broadcasted_iota(jnp.int32, (rows, n), 1) // rows
    for p in range(grid_rows):
        out = jnp.zeros((rows, n), BF16)
        for r in range(blocks):
            goes = target_ref[r] // (blocks * NX * NZ) == p
            first = jnp.where(goes, first_ref[r], n)
            out = jnp.where(column >= first, panel[r * rows:(r + 1) * rows, :], out)
        outgoing[p] = out

    def pcopy(d):
        p = lax.rem(prow + d, grid_rows)
        return pltpu.make_async_remote_copy(
            outgoing.at[p], inc_ref.at[prow], psend.at[d - 1], precv.at[d - 1],
            device_id=(p, pcol), device_id_type=MESH,
        )

    def mcopy(d):
        p = lax.rem(prow + d, grid_rows)
        return pltpu.make_async_remote_copy(
            mark, marks_ref.at[prow], msend.at[d - 1], mrecv.at[d - 1],
            device_id=(p, pcol), device_id_type=MESH,
        )

    for d in range(1, grid_rows):
        mcopy(d).start()
        pcopy(d).start()
    keep_inc = pltpu.make_async_copy(outgoing.at[prow], inc_ref.at[prow], local.at[0])
    keep_inc.start()
    keep_mark = pltpu.make_async_copy(mark, marks_ref.at[prow], local.at[3])
    keep_mark.start()
    keep_diag.wait()
    keep_top.wait()
    diag.across()
    for hop in range(NZ // 2):
        diag.hop(hop)
    diag.finish()
    diag.drain()
    top.start()

    def step(b, carry):
        @pl.when(b == 1)
        def _():
            top.across()
        for hop in range(NZ // 2):
            @pl.when(b == 2 + hop)
            def _():
                top.hop(hop)
        eliminate(b, w, m, t, left, right, hi_ref, lo_ref)
        return carry

    lax.fori_loop(0, n // NB, step, 0)
    top.finish()
    keep_inc.wait()
    keep_mark.wait()
    top.drain()
    for d in range(1, grid_rows):
        mcopy(d).wait()
        pcopy(d).wait()


def factor(first_block, target, diag_one, top_rows, panel_one, grid_rows):
    n = diag_one.shape[1]
    blocks = first_block.shape[0]
    rows = panel_one.shape[0] // blocks
    smem = pl.BlockSpec(memory_space=pltpu.SMEM)
    vmem = pl.BlockSpec(memory_space=pltpu.VMEM)
    anywhere = pl.BlockSpec(memory_space=pl.ANY)
    dma = pltpu.SemaphoreType.DMA
    ring = [dma((NX - 1,)), dma((NX,))] + [dma((NX, 2, NZ // 2))] * 2 + [dma((NX, NZ))] * 2
    return pl.pallas_call(
        factor_kernel,
        out_shape=[
            jax.ShapeDtypeStruct((n, n), BF16),
            jax.ShapeDtypeStruct((n, n), BF16),
            jax.ShapeDtypeStruct((n, n), BF16),
            jax.ShapeDtypeStruct((grid_rows, rows, n), BF16),
            jax.ShapeDtypeStruct((grid_rows, 8, 128), jnp.int32),
        ],
        in_specs=[smem, smem, vmem, vmem, anywhere],
        out_specs=[vmem, vmem, vmem, anywhere, vmem],
        scratch_shapes=[
            pltpu.VMEM((n, n), F32),
            pltpu.VMEM((NB, NB), F32),
            pltpu.VMEM((NB, NB), F32),
            pltpu.VMEM((3 * NB, n), BF16),
            pltpu.VMEM((3 * NB, n), BF16),
            pltpu.VMEM(panel_one.shape, BF16),
            pltpu.VMEM((grid_rows, rows, n), BF16),
            pltpu.VMEM((8, 128), jnp.int32),
            dma((4,)),
        ] + ring + ring + [dma((grid_rows - 1,))] * 4,
        compiler_params=pltpu.CompilerParams(
            collective_id=0, has_side_effects=True, vmem_limit_bytes=32 << 20
        ),
    )(first_block, target, diag_one, top_rows, panel_one)


def ndot(left, right):
    return lax.dot_general(left, right, (((1,), (1,)), ((), ())), preferred_element_type=F32)


def solve_into(rows, hi_ref, lo_ref, store):
    n = hi_ref.shape[0]
    for j in range(n // 256):
        cut = slice(256 * j, 256 * j + 256)
        upto = slice(0, 256 * j + 256)
        part = rows[:, upto]
        out = ndot(part, hi_ref[cut, upto]) + ndot(part, lo_ref[cut, upto])
        store(cut, out.astype(BF16))


def apply_kernel(
    tops, owns, first_ref, marks, hi_ref, lo_ref, top_ref, own_ref, inc_ref, two_ref, diag_ref,
    pf_ref, tf_ref, dn_ref, pn_ref, tf, solved,
):
    i = pl.program_id(0)
    rows, n = top_ref.shape

    @pl.when(i == 0)
    def _():
        pn_ref[...] = two_ref[...].astype(F32)

    @pl.when(i < tops)
    def _():
        at = pl.ds(pl.multiple_of(i * rows, rows), rows)

        def store(cut, value):
            tf[at, cut] = value

        solve_into(top_ref[...], hi_ref, lo_ref, store)

    @pl.when((i >= tops) & (i < tops + owns))
    def _():
        column = lax.broadcasted_iota(jnp.int32, (rows, n), 1)
        x = own_ref[...].astype(F32)
        x = jnp.where(column >= first_ref[i - tops] * rows, x, 0.0).astype(BF16)

        def store(cut, value):
            pf_ref[:, cut] = value

        solve_into(x, hi_ref, lo_ref, store)

    @pl.when(i == tops)
    def _():
        local = tf_ref.shape[0]
        own = tf[pl.ds(pl.multiple_of(lax.axis_index("pcol") * local, local), local), :]
        tf_ref[...] = own
        dn_ref[...] = diag_ref[...] - ndot(own, tf[...])

    @pl.when(i >= tops + owns)
    def _():
        slot = -1
        for r in range(owns):
            to = marks[i - tops - owns, r]
            mine = to // (owns * lax.axis_size("pcol")) == lax.axis_index("prow")
            slot = jnp.where(mine, lax.rem(to, owns), slot)

        @pl.when(slot >= 0)
        def _():
            def store(cut, value):
                solved[:, cut] = value

            solve_into(inc_ref[0], hi_ref, lo_ref, store)
            at = pl.ds(pl.multiple_of(slot * rows, rows), rows)
            update = ndot(solved[...], tf[...]).astype(BF16).astype(F32)
            pn_ref[at, :] = pn_ref[at, :] - update


def apply(first_block, marks, hi, lo, top, own, incoming, two, diag_two):
    n = hi.shape[0]
    sources, rows, _ = incoming.shape
    tops, owns = n // rows, own.shape[0] // rows
    local = diag_two.shape[0]
    fixed = lambda *shape: pl.BlockSpec(shape, lambda i, first, marks: (0,) * len(shape))
    clip = lambda i, low, count: jnp.minimum(jnp.maximum(i - low, 0), count - 1)
    return pl.pallas_call(
        functools.partial(apply_kernel, tops, owns),
        out_shape=[
            jax.ShapeDtypeStruct(own.shape, BF16),
            jax.ShapeDtypeStruct((local, n), BF16),
            jax.ShapeDtypeStruct((local, n), F32),
            jax.ShapeDtypeStruct(two.shape, F32),
        ],
        grid_spec=pltpu.PrefetchScalarGridSpec(
            num_scalar_prefetch=2,
            grid=(tops + owns + sources,),
            in_specs=[
                fixed(n, n), fixed(n, n),
                pl.BlockSpec((rows, n), lambda i, first, marks: (clip(i, 0, tops), 0)),
                pl.BlockSpec((rows, n), lambda i, first, marks: (clip(i, tops, owns), 0)),
                pl.BlockSpec((1, rows, n), lambda i, first, marks: (clip(i, tops + owns, sources), 0, 0)),
                fixed(*two.shape), fixed(local, n),
            ],
            out_specs=[
                pl.BlockSpec((rows, n), lambda i, first, marks: (clip(i, tops, owns), 0)),
                fixed(local, n), fixed(local, n), fixed(*two.shape),
            ],
            scratch_shapes=[pltpu.VMEM((n, n), BF16), pltpu.VMEM((rows, n), BF16)],
        ),
        compiler_params=pltpu.CompilerParams(vmem_limit_bytes=28 << 20),
    )(first_block, marks, hi, lo, top, own, incoming, two, diag_two)


def on_device(diag_one, top_rows, panel_one, first_block, target, diag_two, panel_two):
    hi, lo, tops, incoming, marks = factor(
        first_block, target, diag_one, top_rows, panel_one, lax.axis_size("prow")
    )
    panel_factor, top_own, diag_next, panel_next = apply(
        first_block, marks[:, 0, :2], hi, lo, tops, panel_one, incoming, panel_two, diag_two
    )
    return (panel_factor, top_own, diag_next, panel_next)


def solution(mesh):
    whole = P(("prow", "pcol"), None)
    blocks = P(("prow", "pcol"))
    part = P("pcol", None)
    return jax.shard_map(
        on_device,
        mesh=mesh,
        in_specs=(part, part, whole, blocks, blocks, part, whole),
        out_specs=(whole, part, part, whole),
        check_vma=False,
    )
```

time: 206 us -> 104 us (0.50)
  the two profiles are of different devices: /device:TPU:2 before, /device:TPU:5 now
where the time goes in v1:
time: 104 us; the launch traced here: 103 us
  Pallas kernels  95.1 us (91%)
  local copies, waits for them, and re-layouts  7.62 us (7%)
    pallas_call x1, Pallas kernels, factor(): pl.pallas_call(factor_kernel, out_shape=[jax.ShapeDtypeStruct((n, n), BF1...  71.3 us
    pallas_call x1, Pallas kernels, apply(): pl.pallas_call(functools.partial(apply_kernel, tops, owns), out_shape=[ja...  23.8 us
    unnamed x16, local copies, waits for them, and re-layouts  7.62 us

profile of v1, /device:TPU:5, one launch (start us, length us, event | category | flops | bytes accessed | tf_op | source)
XLA Modules:
  0.0 103.4 jit_solution(16692623241133021339)
XLA Ops:
  0.6 0.0 copy-start
  0.6 1.2 %copy-done = bf16[512,1024]{1,0:T(8,128)(2,1)S(1)} copy-done((bf16[512,1024]{1,0:T(8,128)(2,1)S(1)}, bf16[512,1024]{1,0:T(8,128)(2,1)}, u32[]{:S(2)}) %copy-start) | copy-done | bytes 1048600
  1.9 0.0 copy-start.4
  1.9 0.9 copy-done.4
  2.8 0.0 copy-start.5
  2.8 0.8 copy-done.5
  3.6 0.0 copy-start.6
  3.6 0.7 copy-done.6
  4.3 0.0 copy-start.7
  4.3 0.7 copy-done.7
  4.9 71.3 %shard_map.102 = (bf16[1024,1024]{1,0:T(8,128)(2,1)S(1)}, bf16[1024,1024]{1,0:T(8,128)(2,1)S(1)}, bf16[1024,1024]{1,0:T(8,128)(2,1)S(1)}, bf16[8,256,1024]{2,1,0:T(8,128)(2,1)S(1)}, s32[8,8,128]{2,1,0:T(8,128)S(1)}) custom-call(s32[2]{0:T(128)S(1)} %copy-done.6, s32[2]{0:T(128)S(1)} %copy-done.7, f32[32,1024]{1,0:T(8,128)S(1)} %copy-done.4, ...), custom_call_target="tpu_custom_call" | custom-call | tf_op jit(solution)/shard_map/pallas_call | solution.py:310
  76.2 0.0 copy-start.1
  76.3 1.2 %copy-done.1 = bf16[512,1024]{1,0:T(8,128)(2,1)S(1)} copy-done((bf16[512,1024]{1,0:T(8,128)(2,1)S(1)}, bf16[512,1024]{1,0:T(8,128)(2,1)}, u32[]{:S(2)}) %copy-start.1) | copy-done | bytes 1048600
  77.5 0.0 copy-start.2
  77.5 1.2 %copy-done.2 = bf16[512,1024]{1,0:T(8,128)(2,1)S(1)} copy-done((bf16[512,1024]{1,0:T(8,128)(2,1)S(1)}, bf16[512,1024]{1,0:T(8,128)(2,1)}, u32[]{:S(2)}) %copy-start.2) | copy-done | bytes 1048600
  78.7 0.0 copy-start.3
  78.7 0.9 copy-done.3
  79.6 23.8 %shard_map.103 = (bf16[512,1024]{1,0:T(8,128)(2,1)}, bf16[32,1024]{1,0:T(8,128)(2,1)}, f32[32,1024]{1,0:T(8,128)}, f32[512,1024]{1,0:T(8,128)}) custom-call(s32[2]{0:T(128)S(1)} %copy-done.6, s32[8,2]{1,0:T(8,128)S(1)} %bitcast.1, bf16[1024,1024]{1,0:T(8,128)(2,1)S(1)} %get-tuple-element.10.hi_ref, bf16[1024,1024]{1,0:T(8,128)(2,1)S(1)} %get-tuple-element.11.lo_ref, ...), custom_call_target="tpu_custom_call" | custom-call | tf_op jit(solution)/shard_map/pallas_call | solution.py:416
  (1 shorter events, 0.0 us)
Async XLA Ops:
  0.6 1.2 %copy-start = (bf16[512,1024]{1,0:T(8,128)(2,1)S(1)}, bf16[512,1024]{1,0:T(8,128)(2,1)}, u32[]{:S(2)}) copy-start(bf16[512,1024]{1,0:T(8,128)(2,1)} %own_ref.1) | copy-start | bytes 3145732
  1.9 0.9 copy-start.4
  2.8 0.8 copy-start.5
  3.6 0.7 copy-start.6
  4.3 0.7 copy-start.7
  76.2 1.2 %copy-start.1 = (bf16[512,1024]{1,0:T(8,128)(2,1)S(1)}, bf16[512,1024]{1,0:T(8,128)(2,1)}, u32[]{:S(2)}) copy-start(bf16[512,1024]{1,0:T(8,128)(2,1)} %own_ref.1) | copy-start | bytes 3145732
  77.5 1.2 %copy-start.2 = (bf16[512,1024]{1,0:T(8,128)(2,1)S(1)}, bf16[512,1024]{1,0:T(8,128)(2,1)}, u32[]{:S(2)}) copy-start(bf16[512,1024]{1,0:T(8,128)(2,1)} %two_ref.1) | copy-start | bytes 3145732
  78.7 0.9 copy-start.3

commit v2 on v1

v2 whole, which is shorter than its diff:
```python
import functools

import jax
import jax.numpy as jnp
from jax import lax
from jax.experimental import pallas as pl
from jax.experimental.pallas import tpu as pltpu
from jax.sharding import PartitionSpec as P

F32, BF16 = jnp.float32, jnp.bfloat16
NB = 128


def split2(x):
    hi = x.astype(BF16)
    lo = (x - hi.astype(F32)).astype(BF16)
    return hi, lo


def tdot(left, right):
    return lax.dot_general(left, right, (((0,), (0,)), ((), ())), preferred_element_type=F32)


def row_bcast(x, k):
    return jnp.broadcast_to(x[k:k + 1, :], (8, x.shape[1]))


def factor_block(m_ref, t_ref, G, p, work):
    n = NB
    sub = lax.broadcasted_iota(jnp.int32, (8, n), 0)
    lane = lax.broadcasted_iota(jnp.int32, (8, n), 1)
    groups = n // G
    nch = G // 8
    done = 0
    for s in range(groups):
        r0 = s * G
        band = [m_ref[r0 + 8 * c:r0 + 8 * c + 8, :] for c in range(nch)]
        window = {}
        dvec = [None] * nch

        def spread(j):
            for c in range(j // 8, nch):
                window[j, c] = jnp.broadcast_to(band[c][:, r0 + j:r0 + j + 1], (8, n))

        for j in range(min(p, G)):
            spread(j)
        for k in range(G):
            until = len(work) * (s * G + k + 1) // n
            while done < until:
                work[done]()
                done += 1
            kc, kr = k // 8, k % 8
            piv = row_bcast(window[k, kc], kr)
            dvec[kc] = piv if kr == 0 else jnp.where(sub >= kr, piv, dvec[kc])
            rd = 1.0 / piv
            mult = {c: window[k, c] * rd for c in range(kc, nch)}
            mult[kc] = jnp.where(sub > kr, mult[kc], 0.0)
            for j in range(k + 1, min(k + p, G)):
                jc = j // 8
                other = row_bcast(window[k, jc], j % 8)
                for c in range(jc, nch):
                    window[j, c] = window[j, c] - mult[c] * other
            here = lane == r0 + k
            row = jnp.where(here, 1.0, row_bcast(band[kc], kr))
            for c in range(kc, nch):
                if c == kc:
                    old = jnp.where(here & (sub >= kr), (sub == kr).astype(F32), band[c])
                else:
                    old = jnp.where(here, 0.0, band[c])
                band[c] = old - mult[c] * row
            if k + p < G:
                spread(k + p)
            for c in range(kc, nch):
                del window[k, c]
        for c in range(nch):
            band[c] = band[c] * lax.rsqrt(dvec[c])
            upper = lane > sub + (r0 + 8 * c)
            t_ref[r0 + 8 * c:r0 + 8 * c + 8, :] = jnp.where(upper, 0.0, band[c])
            band[c] = jnp.where(upper & (lane < r0 + G), 0.0, band[c])
        if r0 + G < n:
            r = jnp.concatenate(band, axis=0)
            hi, lo = split2(r)
            prod = tdot(jnp.concatenate([hi, hi, lo], axis=0), jnp.concatenate([hi, lo, hi], axis=0))
            lane_all = lax.broadcasted_iota(jnp.int32, (n - r0 - G, n), 1)
            keep = (lane_all < r0) | (lane_all >= r0 + G)
            m_ref[r0 + G:, :] = jnp.where(keep, m_ref[r0 + G:, :], 0.0) - prod[r0 + G:, :]
    while done < len(work):
        work[done]()
        done += 1


def blk(i, j=None):
    return slice(NB * i, NB * (i + 1 if j is None else j))


def eliminate(w, m, t, left, right, hi_ref, lo_ref, G, p, before, extra):
    n = w.shape[1]
    steps = n // NB

    def update(b, i, start, stop):
        prod = tdot(left[b % 2, :, blk(i)], right[b % 2, :, blk(start, stop)])
        if start == stop - 1 == b:
            w[blk(i), blk(b)] = -prod
        else:
            w[blk(i), blk(start, stop)] = w[blk(i), blk(start, stop)] - prod

    for b in range(steps):
        before(b)
        if b > 0:
            update(b - 1, b, b, b + 1)
        m[...] = w[blk(b), blk(b)]
        work = []
        if b > 0:
            for i in range(b, steps):
                if b > 1:
                    work.append(functools.partial(update, b - 1, i, 0, b - 1))
                work.append(functools.partial(update, b - 1, i, b - 1, b))
                first = max(i, b + 1)
                if first < steps:
                    work.append(functools.partial(update, b - 1, i, first, steps))
        work += extra(b)
        factor_block(m, t, G, p, work)
        th, tl = split2(t[...])
        tt = jnp.concatenate([th, th, tl], axis=1)
        slot = b % 2
        for start, stop in ((0, b), (b, b + 1), (b + 1, steps)):
            if start == stop:
                continue
            cut = blk(start, stop)
            if start == b:
                rh, rl = th, tl
            else:
                wh, wl = split2(w[blk(b), cut])
                r = jnp.dot(tt, jnp.concatenate([wh, wl, wh], axis=0), preferred_element_type=F32)
                rh, rl = split2(r)
            if start > b:
                left[slot, 0:NB, cut] = rh
                left[slot, NB:2 * NB, cut] = rh
                left[slot, 2 * NB:, cut] = rl
            else:
                hi_ref[blk(b), cut] = rh
                lo_ref[blk(b), cut] = rl
            right[slot, 0:NB, cut] = rh
            right[slot, NB:2 * NB, cut] = rl
            right[slot, 2 * NB:, cut] = rh
        if b + 1 < steps:
            hi_ref[blk(b), blk(b + 1, steps)] = jnp.zeros((NB, n - NB * (b + 1)), BF16)
            lo_ref[blk(b), blk(b + 1, steps)] = jnp.zeros((NB, n - NB * (b + 1)), BF16)


NX, NZ = 4, 8
MESH = pl.DeviceIdType.MESH


def ndot(left, right):
    return lax.dot_general(left, right, (((1,), (1,)), ((), ())), preferred_element_type=F32)


def solve_part(rows, hi_ref, lo_ref, j):
    cut, upto = slice(256 * j, 256 * j + 256), slice(0, 256 * j + 256)
    return (ndot(rows[:, upto], hi_ref[cut, upto]) + ndot(rows[:, upto], lo_ref[cut, upto])).astype(BF16)


class Ring:
    def __init__(self, own, whole, sems, trim):
        self.own, self.whole, self.trim = own, whole, trim
        self.xsend, self.xrecv, self.zsend, self.zrecv, self.ssend, self.srecv = sems
        self.rows, self.n = own.shape
        self.prow, pcol = lax.axis_index("prow"), lax.axis_index("pcol")
        self.core = lax.rem(self.prow, 2)
        self.x, self.z = pcol // NZ, lax.rem(pcol, NZ)
        self.sibling = (self.prow + 1 - 2 * self.core, pcol)
        self.hops = (NZ // 2, NZ // 2 - 1)

    def at(self, x, z):
        return (self.prow, lax.rem(x + NX, NX) * NZ + lax.rem(z + NZ, NZ))

    def place(self, xs, zz):
        skip = self.n // NX * xs if self.trim else 0
        width = (self.n - skip) // 2
        row = pl.multiple_of((xs * NZ + zz) * self.rows, self.rows)
        return pl.ds(row, self.rows), pl.ds(pl.multiple_of(skip + self.core * width, 128), width)

    def xcopy(self, xs, d):
        where = self.place(xs, self.z)
        return pltpu.make_async_remote_copy(
            self.own.at[:, where[1]], self.whole.at[where], self.xsend.at[d - 1], self.xrecv.at[xs],
            device_id=self.at(xs + d, self.z), device_id_type=MESH,
        )

    def scopy(self, xs, zz, slot):
        where = self.whole.at[self.place(xs, zz)]
        return pltpu.make_async_remote_copy(
            where, where, self.ssend.at[xs, slot], self.srecv.at[xs, slot],
            device_id=self.sibling, device_id_type=MESH,
        )

    def zcopy(self, xs, zz, way, hop):
        where = self.whole.at[self.place(xs, zz)]
        return pltpu.make_async_remote_copy(
            where, where, self.zsend.at[xs, way, hop], self.zrecv.at[xs, way, hop],
            device_id=self.at(self.x, self.z + 1 - 2 * way), device_id_type=MESH,
        )

    def start(self):
        for xs in range(NX):
            @pl.when(self.x == xs)
            def _():
                for d in range(1, NX):
                    self.xcopy(xs, d).start()

    def across(self):
        for xs in range(NX):
            @pl.when(self.x != xs)
            def _():
                self.xcopy(xs, 1).wait_recv()
            for way in range(2):
                self.zcopy(xs, self.z, way, 0).start()
        for xs in range(NX):
            @pl.when(self.x != xs)
            def _():
                self.scopy(xs, self.z, 0).start()

    def hop(self, hop):
        for way in range(2):
            if hop >= self.hops[way]:
                continue
            back = self.z - hop - 1 if way == 0 else self.z + hop + 1
            back = lax.rem(back + NZ, NZ)
            for xs in range(NX):
                self.zcopy(xs, back, way, hop).wait_recv()
                if hop + 1 < self.hops[way]:
                    self.zcopy(xs, back, way, hop + 1).start()
                self.scopy(xs, back, 1 + hop + way * (NZ // 2)).start()

    def finish(self):
        for xs in range(NX):
            @pl.when(self.x != xs)
            def _():
                self.scopy(xs, self.z, 0).wait_recv()
            for slot in range(1, NZ):
                self.scopy(xs, self.z, slot).wait_recv()

    def drain(self):
        for xs in range(NX):
            @pl.when(self.x == xs)
            def _():
                for d in range(1, NX):
                    self.xcopy(xs, d).wait_send()

            @pl.when(self.x != xs)
            def _():
                self.scopy(xs, self.z, 0).wait_send()
            for way in range(2):
                for hop in range(self.hops[way]):
                    self.zcopy(xs, self.z, way, hop).wait_send()
            for slot in range(1, NZ):
                self.scopy(xs, self.z, slot).wait_send()


class Panels:
    def __init__(self, own, whole, sems):
        self.own, self.whole = own, whole
        self.ysend, self.yrecv, self.fsend, self.frecv, self.ssend, self.srecv = sems
        self.prow, self.pcol = lax.axis_index("prow"), lax.axis_index("pcol")
        self.grid_rows = lax.axis_size("prow")
        self.core = lax.rem(self.prow, 2)

    def row(self, d):
        return lax.rem(self.prow + 2 * d + self.grid_rows, self.grid_rows)

    def copy(self, source, target, send, recv, row):
        return pltpu.make_async_remote_copy(
            source, target, send, recv, device_id=(row, self.pcol), device_id_type=MESH
        )

    def near(self, way, r):
        return self.copy(
            self.own.at[r], self.whole.at[self.prow, r], self.ysend.at[way, r], self.yrecv.at[way, r],
            self.row(1 - 2 * way),
        )

    def far(self, way):
        where = self.whole.at[self.row(2 * way - 1), way]
        return self.copy(where, where, self.fsend.at[way], self.frecv.at[way], self.row(1 - 2 * way))

    def across(self, d, r):
        where = self.whole.at[self.row(d), r]
        source = self.own.at[r] if d == 0 else where
        return self.copy(source, where, self.ssend.at[d, r], self.srecv.at[d, r], self.prow + 1 - 2 * self.core)

    def start(self):
        for r in range(2):
            for way in range(2):
                self.near(way, (r + way) % 2).start()
        for r in range(2):
            self.across(0, r).start()

    def forward(self):
        for way in range(2):
            self.near(way, way).wait_recv()
            self.far(way).start()
            self.across(3 - 2 * way, way).start()

    def pass_on(self):
        for way in range(2):
            self.near(way, 1 - way).wait_recv()
            self.across(3 - 2 * way, 1 - way).start()

    def finish(self):
        for way in range(2):
            self.far(way).wait_recv()
            self.across(2, way).start()
        for d in range(4):
            for r in range(2):
                self.across(d, r).wait()
        for way in range(2):
            self.far(way).wait_send()
            for r in range(2):
                self.near(way, r).wait_send()


def factor_kernel(
    first_ref, target_ref, diag_ref, top_ref, panel_ref,
    hi_ref, lo_ref, tf_ref, pf_ref, inc_ref, marks_ref,
    w, m, t, left, right, tops, masked, mark, local, *sems,
):
    grid_rows, blocks, rows, n = inc_ref.shape
    diag = Ring(diag_ref, w, sems[0:6], True)
    top = Ring(top_ref, tops, sems[6:12], False)
    panels = Panels(panel_ref, inc_ref, sems[12:18])
    msend, mrecv = sems[18:]
    prow, pcol = diag.prow, lax.axis_index("pcol")
    own_rows = pl.ds(pl.multiple_of(pcol * diag.rows, diag.rows), diag.rows)

    barrier = pltpu.get_barrier_semaphore()
    peers = [diag.at(diag.x + d, diag.z) for d in range(1, NX)]
    peers += [diag.at(diag.x, diag.z + 1), diag.at(diag.x, diag.z - 1)]
    peers += [(lax.rem(prow + d, grid_rows), pcol) for d in range(1, grid_rows)]
    for peer in peers:
        pl.semaphore_signal(barrier, inc=1, device_id=peer, device_id_type=MESH)
    keep_diag = pltpu.make_async_copy(diag_ref, w.at[own_rows], local.at[0])
    keep_diag.start()
    keep_top = pltpu.make_async_copy(top_ref, tops.at[own_rows], local.at[1])
    keep_top.start()
    keep_panel = pltpu.make_async_copy(panel_ref, inc_ref.at[prow], local.at[2])
    keep_panel.start()
    lane = lax.broadcasted_iota(jnp.int32, mark.shape, 1)
    word = jnp.where(lane == 0, target_ref[0], target_ref[1])
    for r in range(blocks):
        word = jnp.where(lane == blocks + r, first_ref[r], word)
    mark[...] = word
    pl.semaphore_wait(barrier, len(peers))

    diag.start()

    def mcopy(d):
        return pltpu.make_async_remote_copy(
            mark, marks_ref.at[prow], msend.at[d - 1], mrecv.at[d - 1],
            device_id=(lax.rem(prow + d, grid_rows), pcol), device_id_type=MESH,
        )

    for d in range(1, grid_rows):
        mcopy(d).start()
    keep_mark = pltpu.make_async_copy(mark, marks_ref.at[prow], local.at[3])
    keep_mark.start()
    panels.start()
    keep_diag.wait()
    keep_top.wait()
    keep_panel.wait()
    diag.across()
    for hop in range(NZ // 2):
        diag.hop(hop)
    diag.finish()
    diag.drain()
    top.start()
    column = lax.broadcasted_iota(jnp.int32, (rows, n), 1)
    for r in range(blocks):
        x = inc_ref[prow, r].astype(F32)
        masked[r * rows:(r + 1) * rows, :] = jnp.where(column >= first_ref[r] * rows, x, 0.0).astype(BF16)

    def before(b):
        if b == 1:
            top.across()
        if 2 <= b < 2 + NZ // 2:
            top.hop(b - 2)
        if b == 3:
            panels.forward()
        if b == 5:
            panels.pass_on()
        if b == 6:
            top.finish()

    def solve(x, out, j, piece):
        at = slice(512 * piece, 512 * piece + 512)
        out[at, 256 * j:256 * j + 256] = solve_part(x[at, :], hi_ref, lo_ref, j)

    def extra(b):
        own = {3: [0], 5: [1], 7: [2]}.get(b, [])
        tall = {6: [0, 1], 7: [2]}.get(b, [])
        work = [functools.partial(solve, masked, pf_ref, j, 0) for j in own]
        return work + [functools.partial(solve, tops, tf_ref, j, piece) for j in tall for piece in range(n // 512)]

    eliminate(w, m, t, left, right, hi_ref, lo_ref, 32, 12, before, extra)
    solve(masked, pf_ref, 3, 0)
    for piece in range(n // 512):
        solve(tops, tf_ref, 3, piece)
    panels.finish()
    keep_mark.wait()
    top.drain()
    for d in range(1, grid_rows):
        mcopy(d).wait()


def factor(first_block, target, diag_one, top_rows, panel_one, grid_rows):
    n = diag_one.shape[1]
    blocks = first_block.shape[0]
    rows = panel_one.shape[0] // blocks
    smem = pl.BlockSpec(memory_space=pltpu.SMEM)
    vmem = pl.BlockSpec(memory_space=pltpu.VMEM)
    hbm = pl.BlockSpec(memory_space=pltpu.HBM)
    dma = pltpu.SemaphoreType.DMA
    ring = [dma((NX - 1,)), dma((NX,))] + [dma((NX, 2, NZ // 2))] * 2 + [dma((NX, NZ))] * 2
    here = lambda v: pltpu.with_memory_space_constraint(v, pltpu.HBM)
    return pl.pallas_call(
        factor_kernel,
        out_shape=[
            jax.ShapeDtypeStruct((n, n), BF16),
            jax.ShapeDtypeStruct((n, n), BF16),
            jax.ShapeDtypeStruct((n, n), BF16),
            jax.ShapeDtypeStruct(panel_one.shape, BF16),
            jax.ShapeDtypeStruct((grid_rows, blocks, rows, n), BF16),
            jax.ShapeDtypeStruct((grid_rows, 8, 128), jnp.int32),
        ],
        in_specs=[smem, smem, hbm, hbm, hbm],
        out_specs=[vmem] * 6,
        scratch_shapes=[
            pltpu.VMEM((n, n), F32),
            pltpu.VMEM((NB, NB), F32),
            pltpu.VMEM((NB, NB), F32),
            pltpu.VMEM((2, 3 * NB, n), BF16),
            pltpu.VMEM((2, 3 * NB, n), BF16),
            pltpu.VMEM((n, n), BF16),
            pltpu.VMEM(panel_one.shape, BF16),
            pltpu.VMEM((8, 128), jnp.int32),
            dma((4,)),
        ] + ring + ring
        + [dma((2, 2))] * 2 + [dma((2,))] * 2 + [dma((4, 2))] * 2 + [dma((grid_rows - 1,))] * 2,
        compiler_params=pltpu.CompilerParams(
            collective_id=0, has_side_effects=True, vmem_limit_bytes=24 << 20
        ),
    )(first_block, target, here(diag_one), here(top_rows), here(panel_one.reshape(blocks, rows, n)))


QUAD = 4


def apply_kernel(
    marks, hi_ref, lo_ref, tf_ref, pf_ref, inc_ref, two_ref, diag_ref,
    pf_out, tf_out, dn_out, pn_out, two, diag, acc, x, solved, sems,
):
    sources, blocks, rows, n = inc_ref.shape
    local = diag.shape[0]
    prow, pcol = lax.axis_index("prow"), lax.axis_index("pcol")
    own = pl.ds(pl.multiple_of(pcol * local, local), local)
    load_two = pltpu.make_async_copy(two_ref, two, sems.at[0])
    load_two.start()
    load_diag = pltpu.make_async_copy(diag_ref, diag, sems.at[1])
    load_diag.start()
    save_pf = pltpu.make_async_copy(pf_ref, pf_out, sems.at[2])
    save_pf.start()
    save_tf = pltpu.make_async_copy(tf_ref.at[own], tf_out, sems.at[3])
    save_tf.start()
    load_diag.wait()
    diag[...] = diag[...] - ndot(tf_ref[own, :], tf_ref[...])
    save_dn = pltpu.make_async_copy(diag, dn_out, sems.at[4])
    save_dn.start()
    load_two.wait()
    acc[...] = two[...].astype(F32)
    column = lax.broadcasted_iota(jnp.int32, (rows, n), 1)

    def quad(q, carry):
        slots, some = [], []
        for i in range(QUAD):
            p = q * QUAD + i
            slot, which, here = 0, 0, False
            for r in range(blocks):
                to = marks[p, 0, r]
                mine = to // (blocks * lax.axis_size("pcol")) == prow
                slot = jnp.where(mine, lax.rem(to, blocks), slot)
                which = jnp.where(mine, r, which)
                here = mine | here
            slots.append(slot)
            some.append(here)
            first = jnp.where(here, marks[p, 0, blocks + which] * rows, n)
            x[i * rows:(i + 1) * rows, :] = jnp.where(
                column >= first, inc_ref[p, which].astype(F32), 0.0
            ).astype(BF16)
        anyone = some[0]
        for here in some[1:]:
            anyone = anyone | here

        @pl.when(anyone)
        def _():
            for j in range(n // 256):
                solved[:, 256 * j:256 * j + 256] = solve_part(x, hi_ref, lo_ref, j)
            for j in range(n // 256):
                cut = slice(256 * j, 256 * j + 256)
                update = ndot(solved[...], tf_ref[cut, :]).astype(BF16).astype(F32)
                for i in range(QUAD):
                    at = pl.ds(pl.multiple_of(slots[i] * rows, rows), rows)
                    acc[at, cut] = acc[at, cut] - update[i * rows:(i + 1) * rows, :]

        return carry

    lax.fori_loop(0, sources // QUAD, quad, 0)
    save_pn = pltpu.make_async_copy(acc, pn_out, sems.at[5])
    save_pn.start()
    for save in (save_pf, save_tf, save_dn, save_pn):
        save.wait()


def apply(marks, hi, lo, tf, pf, incoming, two, diag_two):
    n = hi.shape[0]
    rows = incoming.shape[2]
    local = diag_two.shape[0]
    smem = pl.BlockSpec(memory_space=pltpu.SMEM)
    vmem = pl.BlockSpec(memory_space=pltpu.VMEM)
    hbm = pl.BlockSpec(memory_space=pltpu.HBM)
    here = lambda v: pltpu.with_memory_space_constraint(v, pltpu.HBM)
    return pl.pallas_call(
        apply_kernel,
        out_shape=[
            jax.ShapeDtypeStruct(pf.shape, BF16),
            jax.ShapeDtypeStruct((local, n), BF16),
            jax.ShapeDtypeStruct((local, n), F32),
            jax.ShapeDtypeStruct(two.shape, F32),
        ],
        in_specs=[smem, vmem, vmem, vmem, vmem, vmem, hbm, hbm],
        out_specs=[hbm] * 4,
        scratch_shapes=[
            pltpu.VMEM(two.shape, BF16),
            pltpu.VMEM((local, n), F32),
            pltpu.VMEM(two.shape, F32),
            pltpu.VMEM((QUAD * rows, n), BF16),
            pltpu.VMEM((QUAD * rows, n), BF16),
            pltpu.SemaphoreType.DMA((6,)),
        ],
        compiler_params=pltpu.CompilerParams(vmem_limit_bytes=20 << 20),
    )(marks, hi, lo, tf, pf, incoming, here(two), here(diag_two))


def on_device(diag_one, top_rows, panel_one, first_block, target, diag_two, panel_two):
    hi, lo, tf, pf, incoming, marks = factor(
        first_block, target, diag_one, top_rows, panel_one, lax.axis_size("prow")
    )
    return tuple(apply(marks, hi, lo, tf, pf, incoming, panel_two, diag_two))


def solution(mesh):
    whole = P(("prow", "pcol"), None)
    blocks = P(("prow", "pcol"))
    part = P("pcol", None)
    return jax.shard_map(
        on_device,
        mesh=mesh,
        in_specs=(part, part, whole, blocks, blocks, part, whole),
        out_specs=(whole, part, part, whole),
        check_vma=False,
    )
```

time: 104 us -> 92.4 us (0.89)
  the two profiles are of different devices: /device:TPU:5 before, /device:TPU:2 now
where the time goes in v2:
time: 92.4 us; the launch traced here: 90.8 us
  Pallas kernels  88.7 us (96%)
  local copies, waits for them, and re-layouts  1.3 us (1%)
    pallas_call x1, Pallas kernels, factor(): pl.pallas_call(factor_kernel, out_shape=[jax.ShapeDtypeStruct((n, n), BF1...  70.2 us
    pallas_call x1, Pallas kernels, apply(): pl.pallas_call(apply_kernel, out_shape=[jax.ShapeDtypeStruct(pf.shape, BF...  18.5 us

profile of v2, /device:TPU:2, one launch (start us, length us, event | category | flops | bytes accessed | tf_op | source)
XLA Modules:
  0.0 90.8 jit_solution(8052819748318782695)
XLA Ops:
  0.6 0.0 copy-start
  0.6 0.6 copy-done
  1.3 0.0 copy-start.1
  1.3 0.7 copy-done.1
  1.9 70.2 %shard_map.102 = (bf16[1024,1024]{1,0:T(8,128)(2,1)S(1)}, bf16[1024,1024]{1,0:T(8,128)(2,1)S(1)}, bf16[1024,1024]{1,0:T(8,128)(2,1)S(1)}, bf16[512,1024]{1,0:T(8...) custom-call(s32[2]{0:T(128)S(1)} %copy-done, s32[2]{0:T(128)S(1)} %copy-done.1, ...), custom_call_target="tpu_custom_call" | custom-call | tf_op jit(solution)/shard_map/pallas_call | solution.py:425
  72.2 18.5 %shard_map.103 = (bf16[512,1024]{1,0:T(8,128)(2,1)}, bf16[32,1024]{1,0:T(8,128)(2,1)}, f32[32,1024]{1,0:T(8,128)}, f32[512,1024]{1,0:T(8,128)}) custom-call(s32[8,8,128]{2,1,0:T(8,128)S(1)} %get-tuple-element.10.marks, bf16[1024,1024]{1,0:T(8,128)(2,1)S(1)} %get-tuple-element.11.hi_ref, bf16[1024,1024]{1,0:T(8,128)(2,1)S(1)} %get-tuple-element.12.lo_ref, ...), custom_call_target="tpu_custom_call" | custom-call | tf_op jit(solution)/shard_map/pallas_call | solution.py:531
Async XLA Ops:
  0.6 0.7 copy-start
  1.3 0.7 copy-start.1

commit v3 on v2

--- a/solution.py
+++ b/solution.py
@@ -25,7 +25,7 @@
     return jnp.broadcast_to(x[k:k + 1, :], (8, x.shape[1]))
 
 
-def factor_block(m_ref, t_ref, G, p, work):
+def factor_block(m_ref, t_ref, G, p, work, tick):
     n = NB
     sub = lax.broadcasted_iota(jnp.int32, (8, n), 0)
     lane = lax.broadcasted_iota(jnp.int32, (8, n), 1)
@@ -34,6 +34,7 @@
     done = 0
     for s in range(groups):
         r0 = s * G
+        tick(s)
         band = [m_ref[r0 + 8 * c:r0 + 8 * c + 8, :] for c in range(nch)]
         window = {}
         dvec = [None] * nch
@@ -93,36 +94,43 @@
     return slice(NB * i, NB * (i + 1 if j is None else j))
 
 
-def eliminate(w, m, t, left, right, hi_ref, lo_ref, G, p, before, extra):
+def eliminate(w, m, t, left, right, hi_ref, lo_ref, G, p, before, tick, extra):
     n = w.shape[1]
     steps = n // NB
-
-    def update(b, i, start, stop):
-        prod = tdot(left[b % 2, :, blk(i)], right[b % 2, :, blk(start, stop)])
-        if start == stop - 1 == b:
-            w[blk(i), blk(b)] = -prod
+    slots = left.shape[0] // (3 * NB)
+
+    def update(i, k0, k1, start, stop, fresh):
+        at = 3 * NB * (k0 % slots)
+        span = slice(at, at + 3 * NB * (k1 - k0))
+        prod = tdot(left[span, blk(i)], right[span, blk(start, stop)])
+        if fresh:
+            w[blk(i), blk(start, stop)] = -prod
         else:
             w[blk(i), blk(start, stop)] = w[blk(i), blk(start, stop)] - prod
 
     for b in range(steps):
         before(b)
         if b > 0:
-            update(b - 1, b, b, b + 1)
+            update(b, b - 1, b, b, b + 1, False)
         m[...] = w[blk(b), blk(b)]
         work = []
-        if b > 0:
-            for i in range(b, steps):
-                if b > 1:
-                    work.append(functools.partial(update, b - 1, i, 0, b - 1))
-                work.append(functools.partial(update, b - 1, i, b - 1, b))
-                first = max(i, b + 1)
-                if first < steps:
-                    work.append(functools.partial(update, b - 1, i, first, steps))
+        for i in range(b, steps):
+            if b == 0:
+                continue
+            k0 = b - 1
+            if k0 > 0:
+                work.append(functools.partial(update, i, k0, b, 0, k0, False))
+            for c in range(k0, b):
+                work.append(functools.partial(update, i, c, b, c, c + 1, True))
+            first = max(i, b + 1)
+            if first < steps:
+                work.append(functools.partial(update, i, k0, b, first, steps, False))
         work += extra(b)
-        factor_block(m, t, G, p, work)
+        factor_block(m, t, G, p, work, functools.partial(tick, b))
         th, tl = split2(t[...])
         tt = jnp.concatenate([th, th, tl], axis=1)
-        slot = b % 2
+        at = 3 * NB * (b % slots)
+        one, two, three = (slice(at + NB * q, at + NB * q + NB) for q in range(3))
         for start, stop in ((0, b), (b, b + 1), (b + 1, steps)):
             if start == stop:
                 continue
@@ -134,15 +142,15 @@
                 r = jnp.dot(tt, jnp.concatenate([wh, wl, wh], axis=0), preferred_element_type=F32)
                 rh, rl = split2(r)
             if start > b:
-                left[slot, 0:NB, cut] = rh
-                left[slot, NB:2 * NB, cut] = rh
-                left[slot, 2 * NB:, cut] = rl
+                left[one, cut] = rh
+                left[two, cut] = rh
+                left[three, cut] = rl
             else:
                 hi_ref[blk(b), cut] = rh
                 lo_ref[blk(b), cut] = rl
-            right[slot, 0:NB, cut] = rh
-            right[slot, NB:2 * NB, cut] = rl
-            right[slot, 2 * NB:, cut] = rh
+            right[one, cut] = rh
+            right[two, cut] = rl
+            right[three, cut] = rh
         if b + 1 < steps:
             hi_ref[blk(b), blk(b + 1, steps)] = jnp.zeros((NB, n - NB * (b + 1)), BF16)
             lo_ref[blk(b), blk(b + 1, steps)] = jnp.zeros((NB, n - NB * (b + 1)), BF16)
@@ -209,40 +217,40 @@
                 for d in range(1, NX):
                     self.xcopy(xs, d).start()
 
-    def across(self):
-        for xs in range(NX):
+    def across(self, groups):
+        for xs in groups:
             @pl.when(self.x != xs)
             def _():
                 self.xcopy(xs, 1).wait_recv()
             for way in range(2):
                 self.zcopy(xs, self.z, way, 0).start()
-        for xs in range(NX):
+        for xs in groups:
             @pl.when(self.x != xs)
             def _():
                 self.scopy(xs, self.z, 0).start()
 
-    def hop(self, hop):
-        for way in range(2):
-            if hop >= self.hops[way]:
-                continue
-            back = self.z - hop - 1 if way == 0 else self.z + hop + 1
-            back = lax.rem(back + NZ, NZ)
-            for xs in range(NX):
+    def hop(self, hop, groups):
+        for xs in groups:
+            for way in range(2):
+                if hop >= self.hops[way]:
+                    continue
+                back = self.z - hop - 1 if way == 0 else self.z + hop + 1
+                back = lax.rem(back + NZ, NZ)
                 self.zcopy(xs, back, way, hop).wait_recv()
                 if hop + 1 < self.hops[way]:
                     self.zcopy(xs, back, way, hop + 1).start()
                 self.scopy(xs, back, 1 + hop + way * (NZ // 2)).start()
 
-    def finish(self):
-        for xs in range(NX):
+    def finish(self, groups):
+        for xs in groups:
             @pl.when(self.x != xs)
             def _():
                 self.scopy(xs, self.z, 0).wait_recv()
             for slot in range(1, NZ):
                 self.scopy(xs, self.z, slot).wait_recv()
 
-    def drain(self):
-        for xs in range(NX):
+    def drain(self, groups):
+        for xs in groups:
             @pl.when(self.x == xs)
             def _():
                 for d in range(1, NX):
@@ -307,10 +315,12 @@
             self.near(way, 1 - way).wait_recv()
             self.across(3 - 2 * way, 1 - way).start()
 
-    def finish(self):
+    def last(self):
         for way in range(2):
             self.far(way).wait_recv()
             self.across(2, way).start()
+
+    def finish(self):
         for d in range(4):
             for r in range(2):
                 self.across(d, r).wait()
@@ -323,7 +333,7 @@
 def factor_kernel(
     first_ref, target_ref, diag_ref, top_ref, panel_ref,
     hi_ref, lo_ref, tf_ref, pf_ref, inc_ref, marks_ref,
-    w, m, t, left, right, tops, masked, mark, local, *sems,
+    w, m, t, left, right, tops, masked, mark, first, target, local, *sems,
 ):
     grid_rows, blocks, rows, n = inc_ref.shape
     diag = Ring(diag_ref, w, sems[0:6], True)
@@ -345,10 +355,16 @@
     keep_top.start()
     keep_panel = pltpu.make_async_copy(panel_ref, inc_ref.at[prow], local.at[2])
     keep_panel.start()
+    take_first = pltpu.make_async_copy(first_ref, first, local.at[4])
+    take_first.start()
+    take_target = pltpu.make_async_copy(target_ref, target, local.at[5])
+    take_target.start()
+    take_first.wait()
+    take_target.wait()
     lane = lax.broadcasted_iota(jnp.int32, mark.shape, 1)
-    word = jnp.where(lane == 0, target_ref[0], target_ref[1])
+    word = jnp.where(lane == 0, target[0], target[1])
     for r in range(blocks):
-        word = jnp.where(lane == blocks + r, first_ref[r], word)
+        word = jnp.where(lane == blocks + r, first[r], word)
     mark[...] = word
     pl.semaphore_wait(barrier, len(peers))
 
@@ -365,31 +381,37 @@
     keep_mark = pltpu.make_async_copy(mark, marks_ref.at[prow], local.at[3])
     keep_mark.start()
     panels.start()
+    keep_panel.wait()
+    for r in range(blocks):
+        for j in range(n // rows):
+            cut = slice(j * rows, j * rows + rows)
+            piece = inc_ref[prow, r, :, cut]
+            masked[r * rows:(r + 1) * rows, cut] = jnp.where(first[r] <= j, piece, jnp.zeros_like(piece))
+
     keep_diag.wait()
     keep_top.wait()
-    keep_panel.wait()
-    diag.across()
+    every = range(NX)
+    diag.across(every)
+    top.start()
     for hop in range(NZ // 2):
-        diag.hop(hop)
-    diag.finish()
-    diag.drain()
-    top.start()
-    column = lax.broadcasted_iota(jnp.int32, (rows, n), 1)
-    for r in range(blocks):
-        x = inc_ref[prow, r].astype(F32)
-        masked[r * rows:(r + 1) * rows, :] = jnp.where(column >= first_ref[r] * rows, x, 0.0).astype(BF16)
+        diag.hop(hop, every)
+    top.across(every)
+    panels.forward()
+    diag.finish(every)
+    diag.drain(every)
 
     def before(b):
         if b == 1:
-            top.across()
-        if 2 <= b < 2 + NZ // 2:
-            top.hop(b - 2)
-        if b == 3:
-            panels.forward()
+            panels.pass_on()
         if b == 5:
-            panels.pass_on()
+            panels.last()
         if b == 6:
-            top.finish()
+            top.finish(every)
+
+    def tick(b, s):
+        hop = {(1, 0): 0, (2, 1): 1, (3, 2): 2, (4, 3): 3}.get((b, s))
+        if hop is not None:
+            top.hop(hop, every)
 
     def solve(x, out, j, piece):
         at = slice(512 * piece, 512 * piece + 512)
@@ -401,13 +423,13 @@
         work = [functools.partial(solve, masked, pf_ref, j, 0) for j in own]
         return work + [functools.partial(solve, tops, tf_ref, j, piece) for j in tall for piece in range(n // 512)]
 
-    eliminate(w, m, t, left, right, hi_ref, lo_ref, 32, 12, before, extra)
+    eliminate(w, m, t, left, right, hi_ref, lo_ref, 32, 12, before, tick, extra)
     solve(masked, pf_ref, 3, 0)
     for piece in range(n // 512):
         solve(tops, tf_ref, 3, piece)
     panels.finish()
     keep_mark.wait()
-    top.drain()
+    top.drain(every)
     for d in range(1, grid_rows):
         mcopy(d).wait()
 
@@ -416,7 +438,6 @@
     n = diag_one.shape[1]
     blocks = first_block.shape[0]
     rows = panel_one.shape[0] // blocks
-    smem = pl.BlockSpec(memory_space=pltpu.SMEM)
     vmem = pl.BlockSpec(memory_space=pltpu.VMEM)
     hbm = pl.BlockSpec(memory_space=pltpu.HBM)
     dma = pltpu.SemaphoreType.DMA
@@ -432,24 +453,26 @@
             jax.ShapeDtypeStruct((grid_rows, blocks, rows, n), BF16),
             jax.ShapeDtypeStruct((grid_rows, 8, 128), jnp.int32),
         ],
-        in_specs=[smem, smem, hbm, hbm, hbm],
+        in_specs=[hbm] * 5,
         out_specs=[vmem] * 6,
         scratch_shapes=[
             pltpu.VMEM((n, n), F32),
             pltpu.VMEM((NB, NB), F32),
             pltpu.VMEM((NB, NB), F32),
-            pltpu.VMEM((2, 3 * NB, n), BF16),
-            pltpu.VMEM((2, 3 * NB, n), BF16),
+            pltpu.VMEM((2 * 3 * NB, n), BF16),
+            pltpu.VMEM((2 * 3 * NB, n), BF16),
             pltpu.VMEM((n, n), BF16),
             pltpu.VMEM(panel_one.shape, BF16),
             pltpu.VMEM((8, 128), jnp.int32),
-            dma((4,)),
+            pltpu.SMEM(first_block.shape, jnp.int32),
+            pltpu.SMEM(target.shape, jnp.int32),
+            dma((6,)),
         ] + ring + ring
         + [dma((2, 2))] * 2 + [dma((2,))] * 2 + [dma((4, 2))] * 2 + [dma((grid_rows - 1,))] * 2,
         compiler_params=pltpu.CompilerParams(
-            collective_id=0, has_side_effects=True, vmem_limit_bytes=24 << 20
+            collective_id=0, has_side_effects=True, vmem_limit_bytes=28 << 20
         ),
-    )(first_block, target, here(diag_one), here(top_rows), here(panel_one.reshape(blocks, rows, n)))
+    )(here(first_block), here(target), here(diag_one), here(top_rows), here(panel_one.reshape(blocks, rows, n)))
 
 
 QUAD = 4
@@ -477,10 +500,9 @@
     save_dn.start()
     load_two.wait()
     acc[...] = two[...].astype(F32)
-    column = lax.broadcasted_iota(jnp.int32, (rows, n), 1)
 
     def quad(q, carry):
-        slots, some = [], []
+        slots, some, firsts, picks = [], [], [], []
         for i in range(QUAD):
             p = q * QUAD + i
             slot, which, here = 0, 0, False
@@ -492,16 +514,20 @@
                 here = mine | here
             slots.append(slot)
             some.append(here)
-            first = jnp.where(here, marks[p, 0, blocks + which] * rows, n)
-            x[i * rows:(i + 1) * rows, :] = jnp.where(
-                column >= first, inc_ref[p, which].astype(F32), 0.0
-            ).astype(BF16)
+            first = jnp.where(here, marks[p, 0, blocks + which], n)
+            firsts.append(first)
+            picks.append(which)
         anyone = some[0]
         for here in some[1:]:
             anyone = anyone | here
 
         @pl.when(anyone)
         def _():
+            for i in range(QUAD):
+                for j in range(n // rows):
+                    cut = slice(j * rows, j * rows + rows)
+                    piece = inc_ref[q * QUAD + i, picks[i], :, cut]
+                    x[i * rows:(i + 1) * rows, cut] = jnp.where(firsts[i] <= j, piece, jnp.zeros_like(piece))
             for j in range(n // 256):
                 solved[:, 256 * j:256 * j + 256] = solve_part(x, hi_ref, lo_ref, j)
             for j in range(n // 256):

time: 92.4 us -> 84.2 us (0.911)
  Pallas kernels: 88.7 us -> 82.4 us
  local copies, waits for them, and re-layouts: 1.3 us -> 0 us
    pallas_call x1, Pallas kernels: 70.2 us -> 64.5 us  [factor(): pl.pallas_call(factor_kernel, out_shape=[jax.ShapeDtypeStruct((n, n), BF1...]
    unnamed x4 -> x0, local copies, waits for them, and re-layouts: 1.3 us -> none
where the time goes in v3:
time: 84.2 us; the launch traced here: 83.2 us
  Pallas kernels  82.4 us (98%)
    pallas_call x1, Pallas kernels, factor(): pl.pallas_call(factor_kernel, out_shape=[jax.ShapeDtypeStruct((n, n), BF1...  64.5 us
    pallas_call x1, Pallas kernels, apply(): pl.pallas_call(apply_kernel, out_shape=[jax.ShapeDtypeStruct(pf.shape, BF...  17.9 us

profile of v3, /device:TPU:2, one launch (start us, length us, event | category | flops | bytes accessed | tf_op | source)
XLA Modules:
  0.0 83.2 jit_solution(3981211227405859030)
XLA Ops:
  0.6 64.5 %shard_map.102 = (bf16[1024,1024]{1,0:T(8,128)(2,1)S(1)}, bf16[1024,1024]{1,0:T(8,128)(2,1)S(1)}, bf16[1024,1024]{1,0:T(8,128)(2,1)S(1)}, bf16[512,1024]{1,0:T(8...) custom-call(s32[2]{0:T(128)} %first_ref.1, s32[2]{0:T(128)} %target_ref.1, ...), custom_call_target="tpu_custom_call" | custom-call | tf_op jit(solution)/shard_map/pallas_call | solution.py:446
  65.2 17.9 %shard_map.103 = (bf16[512,1024]{1,0:T(8,128)(2,1)}, bf16[32,1024]{1,0:T(8,128)(2,1)}, f32[32,1024]{1,0:T(8,128)}, f32[512,1024]{1,0:T(8,128)}) custom-call(s32[8,8,128]{2,1,0:T(8,128)S(1)} %get-tuple-element.10.marks, bf16[1024,1024]{1,0:T(8,128)(2,1)S(1)} %get-tuple-element.11.hi_ref, bf16[1024,1024]{1,0:T(8,128)(2,1)S(1)} %get-tuple-element.12.lo_ref, ...), custom_call_target="tpu_custom_call" | custom-call | tf_op jit(solution)/shard_map/pallas_call | solution.py:557

commit v4 on v3

--- a/solution.py
+++ b/solution.py
@@ -494,52 +494,48 @@
     save_pf.start()
     save_tf = pltpu.make_async_copy(tf_ref.at[own], tf_out, sems.at[3])
     save_tf.start()
+
+    def place(p):
+        slot, which, first = 0, 0, n
+        for r in range(blocks):
+            to = marks[p, 0, r]
+            mine = to // (blocks * lax.axis_size("pcol")) == prow
+            slot = jnp.where(mine, lax.rem(to, blocks), slot)
+            which = jnp.where(mine, r, which)
+            first = jnp.where(mine, marks[p, 0, blocks + r], first)
+        return slot, which, first
+
+    def solve(q, slots):
+        for i in range(QUAD):
+            slot, which, first = place(q * QUAD + i)
+            slots.append(slot)
+            for j in range(n // rows):
+                cut = slice(j * rows, j * rows + rows)
+                piece = inc_ref[q * QUAD + i, which, :, cut]
+                x[q, i * rows:(i + 1) * rows, cut] = jnp.where(first <= j, piece, jnp.zeros_like(piece))
+        for j in range(n // 256):
+            solved[q, :, 256 * j:256 * j + 256] = solve_part(x.at[q], hi_ref, lo_ref, j)
+
+    def update(q, slots):
+        for j in range(n // 256):
+            cut = slice(256 * j, 256 * j + 256)
+            change = ndot(solved[q], tf_ref[cut, :]).astype(BF16).astype(F32)
+            for i in range(QUAD):
+                at = pl.ds(pl.multiple_of(slots[i] * rows, rows), rows)
+                acc[at, cut] = acc[at, cut] - change[i * rows:(i + 1) * rows, :]
+
+    slots = [[] for _ in range(sources // QUAD)]
+    solve(0, slots[0])
+    load_two.wait()
+    acc[...] = two[...].astype(F32)
     load_diag.wait()
     diag[...] = diag[...] - ndot(tf_ref[own, :], tf_ref[...])
     save_dn = pltpu.make_async_copy(diag, dn_out, sems.at[4])
     save_dn.start()
-    load_two.wait()
-    acc[...] = two[...].astype(F32)
-
-    def quad(q, carry):
-        slots, some, firsts, picks = [], [], [], []
-        for i in range(QUAD):
-            p = q * QUAD + i
-            slot, which, here = 0, 0, False
-            for r in range(blocks):
-                to = marks[p, 0, r]
-                mine = to // (blocks * lax.axis_size("pcol")) == prow
-                slot = jnp.where(mine, lax.rem(to, blocks), slot)
-                which = jnp.where(mine, r, which)
-                here = mine | here
-            slots.append(slot)
-            some.append(here)
-            first = jnp.where(here, marks[p, 0, blocks + which], n)
-            firsts.append(first)
-            picks.append(which)
-        anyone = some[0]
-        for here in some[1:]:
-            anyone = anyone | here
-
-        @pl.when(anyone)
-        def _():
-            for i in range(QUAD):
-                for j in range(n // rows):
-                    cut = slice(j * rows, j * rows + rows)
-                    piece = inc_ref[q * QUAD + i, picks[i], :, cut]
-                    x[i * rows:(i + 1) * rows, cut] = jnp.where(firsts[i] <= j, piece, jnp.zeros_like(piece))
-            for j in range(n // 256):
-                solved[:, 256 * j:256 * j + 256] = solve_part(x, hi_ref, lo_ref, j)
-            for j in range(n // 256):
-                cut = slice(256 * j, 256 * j + 256)
-                update = ndot(solved[...], tf_ref[cut, :]).astype(BF16).astype(F32)
-                for i in range(QUAD):
-                    at = pl.ds(pl.multiple_of(slots[i] * rows, rows), rows)
-                    acc[at, cut] = acc[at, cut] - update[i * rows:(i + 1) * rows, :]
-
-        return carry
-
-    lax.fori_loop(0, sources // QUAD, quad, 0)
+    update(0, slots[0])
+    for q in range(1, sources // QUAD):
+        solve(q, slots[q])
+        update(q, slots[q])
     save_pn = pltpu.make_async_copy(acc, pn_out, sems.at[5])
     save_pn.start()
     for save in (save_pf, save_tf, save_dn, save_pn):
@@ -568,8 +564,8 @@
             pltpu.VMEM(two.shape, BF16),
             pltpu.VMEM((local, n), F32),
             pltpu.VMEM(two.shape, F32),
-            pltpu.VMEM((QUAD * rows, n), BF16),
-            pltpu.VMEM((QUAD * rows, n), BF16),
+            pltpu.VMEM((incoming.shape[0] // QUAD, QUAD * rows, n), BF16),
+            pltpu.VMEM((incoming.shape[0] // QUAD, QUAD * rows, n), BF16),
             pltpu.SemaphoreType.DMA((6,)),
         ],
         compiler_params=pltpu.CompilerParams(vmem_limit_bytes=20 << 20),

time: 84.2 us -> 82.3 us (0.977)
  Pallas kernels: 82.4 us -> 80 us
    pallas_call x1, Pallas kernels: 17.9 us -> 15.4 us  [apply(): pl.pallas_call(apply_kernel, out_shape=[jax.ShapeDtypeStruct(pf.shape, BF...]
where the time goes in v4:
time: 82.3 us; the launch traced here: 80.8 us
  Pallas kernels  80 us (97%)
    pallas_call x1, Pallas kernels, factor(): pl.pallas_call(factor_kernel, out_shape=[jax.ShapeDtypeStruct((n, n), BF1...  64.5 us
    pallas_call x1, Pallas kernels, apply(): pl.pallas_call(apply_kernel, out_shape=[jax.ShapeDtypeStruct(pf.shape, BF...  15.4 us

profile of v4, /device:TPU:2, one launch (start us, length us, event | category | flops | bytes accessed | tf_op | source)
XLA Modules:
  0.0 80.8 jit_solution(14729157088960628674)
XLA Ops:
  0.6 64.5 %shard_map.102 = (bf16[1024,1024]{1,0:T(8,128)(2,1)S(1)}, bf16[1024,1024]{1,0:T(8,128)(2,1)S(1)}, bf16[1024,1024]{1,0:T(8,128)(2,1)S(1)}, bf16[512,1024]{1,0:T(8...) custom-call(s32[2]{0:T(128)} %first_ref.1, s32[2]{0:T(128)} %target_ref.1, ...), custom_call_target="tpu_custom_call" | custom-call | tf_op jit(solution)/shard_map/pallas_call | solution.py:446
  65.2 15.4 %shard_map.103 = (bf16[512,1024]{1,0:T(8,128)(2,1)}, bf16[32,1024]{1,0:T(8,128)(2,1)}, f32[32,1024]{1,0:T(8,128)}, f32[512,1024]{1,0:T(8,128)}) custom-call(s32[8,8,128]{2,1,0:T(8,128)S(1)} %get-tuple-element.10.marks, bf16[1024,1024]{1,0:T(8,128)(2,1)S(1)} %get-tuple-element.11.hi_ref, bf16[1024,1024]{1,0:T(8,128)(2,1)S(1)} %get-tuple-element.12.lo_ref, ...), custom_call_target="tpu_custom_call" | custom-call | tf_op jit(solution)/shard_map/pallas_call | solution.py:553
